TPU v7x, 32 devices: a whole 2x2x4 slice. The times are simulated.
32 devices in a mesh: dp: 16 (over z, x, core), seq: 2 (over y).
Axes of the slice: x: 2, y: 2, z: 4, core: 2. Of those that a mesh axis runs over, the one named last changes fastest.
Arguments:
- images: bfloat16 [32, 592, 1024], P('dp', 'seq'), may hold values from -6 to 6
- cotangent: bfloat16 [32, 592, 1024], P('dp', 'seq'), may hold values from -6 to 6
- w_qkv: float32 [1024, 3072], P('dp', 'seq'), may hold values from -0.1875 to 0.1875
- w_out: float32 [1024, 1024], P('dp', 'seq'), may hold values from -1 to 1
- w_up: float32 [1024, 4096], P('dp', 'seq'), may hold values from -0.1875 to 0.1875
- w_down: float32 [4096, 1024], P('dp', 'seq'), may hold values from -0.09375 to 0.09375
- gains: float32 [2, 1024], P(None, ('dp', 'seq')), may hold values from 0.5 to 1.5
- biases: float32 [10, 1024], P(None, ('dp', 'seq')), may hold values from -3 to 3
- first_qkv: float32 [1024, 3072], P('dp', 'seq'), may hold values from -120 to 120
- first_out: float32 [1024, 1024], P('dp', 'seq'), may hold values from -120 to 120
- first_up: float32 [1024, 4096], P('dp', 'seq'), may hold values from -120 to 120
- first_down: float32 [4096, 1024], P('dp', 'seq'), may hold values from -120 to 120
- first_gains: float32 [2, 1024], P(None, ('dp', 'seq')), may hold values from -120 to 120
- first_biases: float32 [10, 1024], P(None, ('dp', 'seq')), may hold values from -120 to 120
- second_qkv: float32 [1024, 3072], P('dp', 'seq'), may hold values from 100 to 10000
- second_out: float32 [1024, 1024], P('dp', 'seq'), may hold values from 100 to 10000
- second_up: float32 [1024, 4096], P('dp', 'seq'), may hold values from 100 to 10000
- second_down: float32 [4096, 1024], P('dp', 'seq'), may hold values from 100 to 10000
- second_gains: float32 [2, 1024], P(None, ('dp', 'seq')), may hold values from 100 to 10000
- second_biases: float32 [10, 1024], P(None, ('dp', 'seq')), may hold values from 100 to 10000
Outputs:
- out_images: bfloat16 [32, 592, 1024], P('dp', 'seq')
- grad_images: bfloat16 [32, 592, 1024], P('dp', 'seq')
- grad_qkv: float32 [1024, 3072], P('dp', 'seq')
- grad_out: float32 [1024, 1024], P('dp', 'seq')
- grad_up: float32 [1024, 4096], P('dp', 'seq')
- grad_down: float32 [4096, 1024], P('dp', 'seq')
- grad_gains: float32 [2, 1024], P(None, ('dp', 'seq'))
- grad_biases: float32 [10, 1024], P(None, ('dp', 'seq'))
- new_qkv: float32 [1024, 3072], P('dp', 'seq')
- new_out: float32 [1024, 1024], P('dp', 'seq')
- new_up: float32 [1024, 4096], P('dp', 'seq')
- new_down: float32 [4096, 1024], P('dp', 'seq')
- new_gains: float32 [2, 1024], P(None, ('dp', 'seq'))
- new_biases: float32 [10, 1024], P(None, ('dp', 'seq'))
- new_first_qkv: float32 [1024, 3072], P('dp', 'seq')
- new_first_out: float32 [1024, 1024], P('dp', 'seq')
- new_first_up: float32 [1024, 4096], P('dp', 'seq')
- new_first_down: float32 [4096, 1024], P('dp', 'seq')
- new_first_gains: float32 [2, 1024], P(None, ('dp', 'seq'))
- new_first_biases: float32 [10, 1024], P(None, ('dp', 'seq'))
- new_second_qkv: float32 [1024, 3072], P('dp', 'seq')
- new_second_out: float32 [1024, 1024], P('dp', 'seq')
- new_second_up: float32 [1024, 4096], P('dp', 'seq')
- new_second_down: float32 [4096, 1024], P('dp', 'seq')
- new_second_gains: float32 [2, 1024], P(None, ('dp', 'seq'))
- new_second_biases: float32 [10, 1024], P(None, ('dp', 'seq'))
All inputs are finite; a program needn't handle non-finite values.
Results may differ from a plain program's by a relative error of at most 0.028.
Values may be sent and summed in bfloat16 or wider, within the bound.
A program may use at most 256 MiB of HBM per device.

v0:
```python
import jax
import jax.numpy as jnp
from jax import lax
from jax.sharding import PartitionSpec as P

HEAD_DIM = 64
PATCH_TOK = 577
STEP = 5


def normalize(rows):
    center = rows - jnp.mean(rows, axis=-1, keepdims=True)
    inverse = lax.rsqrt(jnp.mean(center * center, axis=-1, keepdims=True) + 1e-06)
    return (center * inverse, inverse)


def norm_back(grad_out, normed, inverse, gain):
    scaled = grad_out * gain
    return inverse * (
        scaled
        - jnp.mean(scaled, axis=-1, keepdims=True)
        - normed * jnp.mean(scaled * normed, axis=-1, keepdims=True)
    )


def gelu_value(pre):
    return pre * 0.5 * (1.0 + lax.erf(pre * 0.7071067811865476))


def gelu_slope(pre):
    return (
        0.5 * (1.0 + lax.erf(pre * 0.7071067811865476))
        + pre * jnp.exp(-0.5 * pre * pre) * 0.3989422804014327
    )


def adamw(param, grad, first, second):
    first_new = 0.9 * first + 0.1 * grad
    second_new = 0.95 * second + 0.05 * grad * grad
    step_size = first_new / (1.0 - 0.9**STEP) / (jnp.sqrt(second_new / (1.0 - 0.95**STEP)) + 1e-08)
    return (param - 0.004 * (step_size + 0.05 * param), first_new, second_new)


def body(
    images,
    cotangent,
    w_qkv,
    w_out,
    w_up,
    w_down,
    gains,
    biases,
    first_qkv,
    first_out,
    first_up,
    first_down,
    first_gains,
    first_biases,
    second_qkv,
    second_out,
    second_up,
    second_down,
    second_gains,
    second_biases,
):
    params = (w_qkv, w_out, w_up, w_down, gains, biases)
    firsts = (first_qkv, first_out, first_up, first_down, first_gains, first_biases)
    seconds = (second_qkv, second_out, second_up, second_down, second_gains, second_biases)
    kernels = tuple((param.astype(jnp.bfloat16) for param in params))
    block_parts = (
        lax.all_gather(kernels[0], "seq", axis=1, tiled=True),
        lax.all_gather(kernels[1], "seq", axis=1, tiled=True),
        lax.all_gather(kernels[2], "seq", axis=1, tiled=True),
        lax.all_gather(kernels[3], "seq", axis=1, tiled=True),
        lax.all_gather(kernels[4], "seq", axis=1, tiled=True),
        lax.all_gather(kernels[5], "seq", axis=1, tiled=True),
    )
    wide_qkv, wide_out, wide_up, wide_down, wide_gains, wide_biases = (
        lax.all_gather(block_parts[0], "dp", axis=0, tiled=True),
        lax.all_gather(block_parts[1], "dp", axis=0, tiled=True),
        lax.all_gather(block_parts[2], "dp", axis=0, tiled=True),
        lax.all_gather(block_parts[3], "dp", axis=0, tiled=True),
        lax.all_gather(block_parts[4], "dp", axis=1, tiled=True),
        lax.all_gather(block_parts[5], "dp", axis=1, tiled=True),
    )
    count, group, width = images.shape
    heads = width // HEAD_DIM
    scale = HEAD_DIM ** (-0.5)
    pad_len = group * lax.axis_size("seq")
    offset = lax.axis_index("seq") * group
    query_live = offset + jnp.arange(group, dtype=jnp.int32) < PATCH_TOK
    key_live = jnp.arange(pad_len, dtype=jnp.int32) < PATCH_TOK
    gain = wide_gains.astype(jnp.float32)
    bias = wide_biases.astype(jnp.float32)
    rows = images.astype(jnp.float32)
    normed_a, inverse_a = normalize(rows)
    hidden_a = (normed_a * gain[0] + bias[0]).astype(jnp.bfloat16)
    mixed = jnp.einsum("icd,de->ice", hidden_a, wide_qkv, preferred_element_type=jnp.float32)
    queries = (mixed[..., :width] + bias[1]).astype(jnp.bfloat16)
    keys = mixed[..., width : 2 * width].astype(jnp.bfloat16)
    values = (mixed[..., 2 * width :] + bias[2]).astype(jnp.bfloat16)
    keys_all, values_all = (
        lax.all_gather(keys, "seq", axis=1, tiled=True),
        lax.all_gather(values, "seq", axis=1, tiled=True),
    )
    query_heads = queries.reshape(count, group, heads, HEAD_DIM)
    key_heads = keys_all.reshape(count, pad_len, heads, HEAD_DIM)
    value_heads = values_all.reshape(count, pad_len, heads, HEAD_DIM)

    def score_block():
        scores = (
            jnp.einsum(
                "ichd,ishd->ihcs", query_heads, key_heads, preferred_element_type=jnp.float32
            )
            * scale
        )
        return jnp.where(key_live[None, None, None, :], scores, -1e30)

    scores = score_block()
    top = jnp.max(scores, axis=-1, keepdims=True)
    lse = top + jnp.log(jnp.sum(jnp.exp(scores - top), axis=-1, keepdims=True))
    probs_b = jnp.exp(scores - lse).astype(jnp.bfloat16)
    context = (
        jnp.einsum("ihcs,ishd->ichd", probs_b, value_heads, preferred_element_type=jnp.float32)
        .reshape(count, group, width)
        .astype(jnp.bfloat16)
    )
    resid = (
        rows
        + jnp.einsum("icd,de->ice", context, wide_out, preferred_element_type=jnp.float32)
        + bias[3]
    )
    normed_b, inverse_b = normalize(resid)
    hidden_b = (normed_b * gain[1] + bias[4]).astype(jnp.bfloat16)
    pre = jnp.einsum("icd,df->icf", hidden_b, wide_up, preferred_element_type=jnp.float32) + bias[
        6:
    ].reshape(-1)
    active = gelu_value(pre).astype(jnp.bfloat16)
    out_images = (
        resid
        + jnp.einsum("icf,fd->icd", active, wide_down, preferred_element_type=jnp.float32)
        + bias[5]
    ).astype(jnp.bfloat16)
    back_qkv, back_out, back_up, back_down, back_gains = (
        wide_qkv,
        wide_out,
        wide_up,
        wide_down,
        wide_gains,
    )
    back_gain = back_gains.astype(jnp.float32)
    grad_y = cotangent.astype(jnp.float32) * query_live[None, :, None].astype(jnp.float32)
    grad_yb = grad_y.astype(jnp.bfloat16)
    g_down = jnp.einsum("icf,icd->fd", active, grad_yb, preferred_element_type=jnp.float32)
    grad_pre = jnp.einsum(
        "icd,fd->icf", grad_yb, back_down, preferred_element_type=jnp.float32
    ) * gelu_slope(pre)
    grad_preb = grad_pre.astype(jnp.bfloat16)
    g_up = jnp.einsum("icd,icf->df", hidden_b, grad_preb, preferred_element_type=jnp.float32)
    grad_hb = jnp.einsum("icf,df->icd", grad_preb, back_up, preferred_element_type=jnp.float32)
    grad_resid = grad_y + norm_back(grad_hb, normed_b, inverse_b, back_gain[1])
    grad_rb = grad_resid.astype(jnp.bfloat16)
    g_outw = jnp.einsum("icd,ice->de", context, grad_rb, preferred_element_type=jnp.float32)
    grad_ctx = (
        jnp.einsum("ice,de->icd", grad_rb, back_out, preferred_element_type=jnp.float32)
        .astype(jnp.bfloat16)
        .reshape(count, group, heads, HEAD_DIM)
    )
    probs = jnp.exp(score_block() - lse)
    grad_probs = jnp.einsum(
        "ichd,ishd->ihcs", grad_ctx, value_heads, preferred_element_type=jnp.float32
    )
    part_v = jnp.einsum(
        "ihcs,ichd->ishd", probs.astype(jnp.bfloat16), grad_ctx, preferred_element_type=jnp.float32
    ).reshape(count, pad_len, width)
    delta = jnp.sum(probs * grad_probs, axis=-1, keepdims=True)
    grad_scores = (probs * (grad_probs - delta) * scale).astype(jnp.bfloat16)
    grad_q = jnp.einsum(
        "ihcs,ishd->ichd", grad_scores, key_heads, preferred_element_type=jnp.float32
    ).reshape(count, group, width)
    part_k = jnp.einsum(
        "ihcs,ichd->ishd", grad_scores, query_heads, preferred_element_type=jnp.float32
    ).reshape(count, pad_len, width)
    grad_k, grad_v = (
        lax.psum_scatter(
            part_k.astype(jnp.bfloat16), "seq", scatter_dimension=1, tiled=True
        ).astype(jnp.float32),
        lax.psum_scatter(
            part_v.astype(jnp.bfloat16), "seq", scatter_dimension=1, tiled=True
        ).astype(jnp.float32),
    )
    grad_mixed = jnp.concatenate([grad_q, grad_k, grad_v], axis=-1).astype(jnp.bfloat16)
    g_qkv = jnp.einsum("icd,ice->de", hidden_a, grad_mixed, preferred_element_type=jnp.float32)
    grad_ha = jnp.einsum("ice,de->icd", grad_mixed, back_qkv, preferred_element_type=jnp.float32)
    grad_images = (grad_resid + norm_back(grad_ha, normed_a, inverse_a, back_gain[0])).astype(
        jnp.bfloat16
    )
    g_gains = jnp.stack(
        [jnp.sum(grad_ha * normed_a, axis=(0, 1)), jnp.sum(grad_hb * normed_b, axis=(0, 1))]
    )
    g_biases = jnp.concatenate(
        [
            jnp.stack(
                [
                    jnp.sum(grad_ha, axis=(0, 1)),
                    jnp.sum(grad_q, axis=(0, 1)),
                    jnp.sum(grad_v, axis=(0, 1)),
                    jnp.sum(grad_resid, axis=(0, 1)),
                    jnp.sum(grad_hb, axis=(0, 1)),
                    jnp.sum(grad_y, axis=(0, 1)),
                ]
            ),
            jnp.sum(grad_pre, axis=(0, 1)).reshape(-1, width),
        ],
        axis=0,
    )
    partial_sums = (
        lax.psum_scatter(g_qkv.astype(jnp.bfloat16), "dp", scatter_dimension=0, tiled=True).astype(
            jnp.float32
        ),
        lax.psum_scatter(g_outw.astype(jnp.bfloat16), "dp", scatter_dimension=0, tiled=True).astype(
            jnp.float32
        ),
        lax.psum_scatter(g_up.astype(jnp.bfloat16), "dp", scatter_dimension=0, tiled=True).astype(
            jnp.float32
        ),
        lax.psum_scatter(g_down.astype(jnp.bfloat16), "dp", scatter_dimension=0, tiled=True).astype(
            jnp.float32
        ),
        lax.psum_scatter(
            g_gains.astype(jnp.bfloat16), "dp", scatter_dimension=1, tiled=True
        ).astype(jnp.float32),
        lax.psum_scatter(
            g_biases.astype(jnp.bfloat16), "dp", scatter_dimension=1, tiled=True
        ).astype(jnp.float32),
    )
    totals = (
        lax.psum_scatter(
            partial_sums[0].astype(jnp.bfloat16), "seq", scatter_dimension=1, tiled=True
        ).astype(jnp.float32),
        lax.psum_scatter(
            partial_sums[1].astype(jnp.bfloat16), "seq", scatter_dimension=1, tiled=True
        ).astype(jnp.float32),
        lax.psum_scatter(
            partial_sums[2].astype(jnp.bfloat16), "seq", scatter_dimension=1, tiled=True
        ).astype(jnp.float32),
        lax.psum_scatter(
            partial_sums[3].astype(jnp.bfloat16), "seq", scatter_dimension=1, tiled=True
        ).astype(jnp.float32),
        lax.psum_scatter(
            partial_sums[4].astype(jnp.bfloat16), "seq", scatter_dimension=1, tiled=True
        ).astype(jnp.float32),
        lax.psum_scatter(
            partial_sums[5].astype(jnp.bfloat16), "seq", scatter_dimension=1, tiled=True
        ).astype(jnp.float32),
    )
    updated = [
        adamw(param, grad, first, second)
        for param, grad, first, second in zip(params, totals, firsts, seconds)
    ]
    news = tuple((entry[0] for entry in updated))
    new_firsts = tuple((entry[1] for entry in updated))
    new_seconds = tuple((entry[2] for entry in updated))
    return (
        out_images,
        grad_images,
        totals[0],
        totals[1],
        totals[2],
        totals[3],
        totals[4],
        totals[5],
        news[0],
        news[1],
        news[2],
        news[3],
        news[4],
        news[5],
        new_firsts[0],
        new_firsts[1],
        new_firsts[2],
        new_firsts[3],
        new_firsts[4],
        new_firsts[5],
        new_seconds[0],
        new_seconds[1],
        new_seconds[2],
        new_seconds[3],
        new_seconds[4],
        new_seconds[5],
    )


def solution(mesh):
    return jax.shard_map(
        body,
        mesh=mesh,
        in_specs=(
            P("dp", "seq", None),
            P("dp", "seq", None),
            P("dp", "seq"),
            P("dp", "seq"),
            P("dp", "seq"),
            P("dp", "seq"),
            P(None, ("dp", "seq")),
            P(None, ("dp", "seq")),
            P("dp", "seq"),
            P("dp", "seq"),
            P("dp", "seq"),
            P("dp", "seq"),
            P(None, ("dp", "seq")),
            P(None, ("dp", "seq")),
            P("dp", "seq"),
            P("dp", "seq"),
            P("dp", "seq"),
            P("dp", "seq"),
            P(None, ("dp", "seq")),
            P(None, ("dp", "seq")),
        ),
        out_specs=(
            P("dp", "seq", None),
            P("dp", "seq", None),
            P("dp", "seq"),
            P("dp", "seq"),
            P("dp", "seq"),
            P("dp", "seq"),
            P(None, ("dp", "seq")),
            P(None, ("dp", "seq")),
            P("dp", "seq"),
            P("dp", "seq"),
            P("dp", "seq"),
            P("dp", "seq"),
            P(None, ("dp", "seq")),
            P(None, ("dp", "seq")),
            P("dp", "seq"),
            P("dp", "seq"),
            P("dp", "seq"),
            P("dp", "seq"),
            P(None, ("dp", "seq")),
            P(None, ("dp", "seq")),
            P("dp", "seq"),
            P("dp", "seq"),
            P("dp", "seq"),
            P("dp", "seq"),
            P(None, ("dp", "seq")),
            P(None, ("dp", "seq")),
        ),
        check_vma=False,
    )
```

profile of v0, /device:TPU:0, one launch (start us, length us, event | category | flops | bytes accessed | tf_op | source)
XLA Modules:
  0.0 1155.0 jit_solution(3185854335412844673)
XLA Ops:
  8.4 8.7 all_gather.46
  17.8 4.3 all-gather.2
  22.2 22.7 %all-gather.3 = bf16[16,64,10]{1,2,0:T(8,128)(2,1)S(1)} all-gather(bf16[1,64,10]{1,2,0:T(8,128)(2,1)S(1)} %reshape.162), channel_id=1, replica_groups=mesh['dp'=16,'seq'=2] {'dp'}, dimensions={0}, use_global_device_ids=true | all-gather | bytes 21760 | tf_op jit(solution)/shard_map/all_gather | solution.py:84
  45.7 4.2 all-gather
  50.0 17.9 %all-gather.1 = bf16[16,64,2]{1,2,0:T(2,128)(2,1)S(1)} all-gather(bf16[1,64,2]{1,2,0:T(2,128)(2,1)S(1)} %reshape.158), channel_id=1, replica_groups=mesh['dp'=16,'seq'=2] {'dp'}, dimensions={0}, use_global_device_ids=true | all-gather | bytes 4352 | tf_op jit(solution)/shard_map/all_gather | solution.py:83
  69.4 10.9 all-gather.11.cloned.1.call-done
  80.3 6.6 fusion.31
  87.0 2.6 fusion.49
  90.8 3.0 slice.71
  93.9 5.0 all_gather.50
  99.1 14.9 %all_gather.52 = bf16[64,4096]{1,0:T(8,128)(2,1)} all-gather(bf16[64,2048]{1,0:T(8,128)(2,1)S(1)} %convert_element_type.171), channel_id=1, replica_groups=mesh['dp'=16,'seq'=2] {'seq'}, dimensions={1}, use_global_device_ids=true | all-gather | bytes 786432 | tf_op jit(solution)/shard_map/all_gather | solution.py:73
  114.4 1.8 copy.103
  116.3 15.7 %all-gather.13.cloned.1.call-done = bf16[2,592,1024]{2,1,0:T(8,128)(2,1)} async-done(((bf16[2,296,1024]{2,1,0:T(8,128)(2,1)}), bf16[2,592,1024]{2,1,0:T(8,128)(2,1)}) %all-gather.13.cloned.1.call-update) | async-done | bytes 2424848 | tf_op jit(solution)/shard_map/all_gather | solution.py:104
  132.0 4.4 copy.102
  136.4 33.9 %all-gather.15.cloned.1.call-done = bf16[2,592,1024]{2,1,0:T(8,128)(2,1)} async-done(((bf16[2,296,1024]{2,1,0:T(8,128)(2,1)}), bf16[2,592,1024]{2,1,0:T(8,128)(2,1)}) %all-gather.15.cloned.1.call-update) | async-done | bytes 2424848 | tf_op jit(solution)/shard_map/all_gather | solution.py:103
  170.3 4.4 copy.104
  174.7 14.2 %fusion.2 = (f32[2,16,296]{2,1,0:T(8,128)S(1)}, f32[2,16,296,592]{3,2,1,0:T(8,128)}) fusion(pred[592]{0:T(1024)(128)(4,1)S(1)} %iota_compare_fusion, bf16[2,296,16,64]{1,3,2,0:T(8,128)(2,1)S(1)} %bitcast.138, bf16[2,592,16,64]{1,3,2,0:T(8,128)(2,1)} %bitcast.130), kind=kOutput, calls=%fused_computation.7 | convolution fusion | flops 734563072 | bytes 26105424 | tf_op jit(solution)/shard_map/ichd,ishd->ihcs/dot_general | solution.py:112
  188.9 9.5 exponential_reduce_fusion
  198.4 10.8 convolution_convert_fusion.1
  209.1 4.7 all-gather.17.cloned.1.call-done
  213.8 3.3 fusion.109
  219.1 69.8 %all-gather.19.cloned.1.call-done = bf16[1024,4096]{1,0:T(8,128)(2,1)} async-done(((bf16[64,4096]{1,0:T(8,128)(2,1)}), bf16[1024,4096]{1,0:T(8,128)(2,1)}) %all-gather.19.cloned.1.call-update) | async-done | bytes 8388624 | tf_op jit(solution)/shard_map/all_gather | solution.py:81
  288.9 12.3 %multiply_convert_fusion.1 = (bf16[2,296,4096]{2,1,0:T(8,128)(2,1)S(1)}, f32[2,296,4096]{2,1,0:T(8,128)}) fusion(f32[4096]{0:T(1024)S(1)} %bitcast.159, bf16[1024,4096]{1,0:T(8,128)(2,1)} %all-gather.19.cloned.1.call-done, f32[2,296,1024]{2,1,0:T(8,128)} %copy-done.3, f32[1024]{0:T(1024)S(1)} %bitcast.166, f32[1024]{0:T(1024)S(1)} %bitcast.155, ...), kind=kOutput, calls=%fused_computation.21 | convolution fusion | flops 4983635968 | bytes 25391744 | tf_op jit(solution)/shard_map/icd,df->icf/dot_general | solution.py:135
  301.2 2.2 copy-done.48
  303.4 9.2 bitcast_convert_fusion
  312.7 102.2 %reduce-scatter.39.cloned.1.call-done = bf16[256,1024]{1,0:T(8,128)(2,1)} async-done(((bf16[4096,1024]{1,0:T(8,128)(2,1)}), bf16[256,1024]{1,0:T(8,128)(2,1)}) %reduce-scatter.39.cloned.1.call-update) | async-done | bytes 524304 | tf_op jit(solution)/shard_map/reduce_scatter | solution.py:227
  414.9 16.5 %reduce-scatter.41.cloned.1.call-done = bf16[256,512]{1,0:T(8,128)(2,1)} async-done(((bf16[256,1024]{1,0:T(8,128)(2,1)}), bf16[256,512]{1,0:T(8,128)(2,1)}) %reduce-scatter.41.cloned.1.call-update) | async-done | bytes 262160 | tf_op jit(solution)/shard_map/reduce_scatter | solution.py:247
  431.4 2.6 multiply_subtract_fusion
  434.0 8.6 all_gather.54
  442.7 74.4 %all-gather.21.cloned.1.call-done = bf16[4096,1024]{1,0:T(8,128)(2,1)} async-done(((bf16[256,1024]{1,0:T(8,128)(2,1)}), bf16[4096,1024]{1,0:T(8,128)(2,1)}) %all-gather.21.cloned.1.call-update) | async-done | bytes 8388624 | tf_op jit(solution)/shard_map/all_gather | solution.py:82
  517.1 12.6 %fusion.112 = (bf16[4096]{0:T(1024)(128)(2,1)S(1)}, bf16[2,296,4096]{2,1,0:T(8,128)(2,1)S(1)}) fusion(f32[2,296,4096]{2,1,0:T(8,128)} %get-tuple-element.77, f32[4096]{0:T(1024)S(1)} %bitcast.160, bf16[4096,1024]{1,0:T(8,128)(2,1)} %all-gather.21.cloned.1.call-done, bf16[2,296,1024]{2,1,0:T(8,128)(2,1)S(1)} %copy-done.13, f32[296]{0:T(512)} %copy-done.32), kind=kOutput, calls=%fused_computation.148 | convolution fusion | flops 4996968448 | bytes 24175776 | tf_op jit(solution)/shard_map/icd,fd->icf/dot_general | solution.py:155
  529.7 10.3 multiply_reduce_fusion.1
  542.8 2.5 fusion.64
  545.3 1.8 copy.106
  547.1 12.0 %convolution_convert_fusion = bf16[2,16,64,592]{3,2,1,0:T(8,128)(2,1)} fusion(bf16[2,296,16,64]{1,3,2,0:T(8,128)(2,1)S(1)} %bitcast.136, f32[2,16,296]{2,1,0:T(8,128)S(1)} %log_add_fusion, f32[2,16,296,592]{3,2,1,0:T(8,128)} %get-tuple-element.73, pred[592]{0:T(1024)(128)(4,1)S(1)} %iota_compare_fusion), kind=kOutput, calls=%fused_computation.83 | convolution fusion | flops 741392384 | bytes 26105424 | tf_op jit(solution)/shard_map/ihcs,ichd->ishd/dot_general | solution.py:173
  559.1 6.5 copy.115
  565.6 3.9 copy.130
  569.8 13.8 %fusion.113 = f32[2,16,296,592]{3,2,1,0:T(8,128)} fusion(bf16[2,296,16,64]{1,3,2,0:T(8,128)(2,1)S(1)} %bitcast.137, bf16[2,592,16,64]{1,3,2,0:T(8,128)(2,1)} %bitcast.128), kind=kOutput, calls=%fused_computation.149 | convolution fusion | flops 717750272 | bytes 26066944 | tf_op jit(solution)/shard_map/ichd,ishd->ihcs/dot_general | solution.py:170
  583.6 70.8 %fusion.59 = bf16[2,16,64,592]{3,2,1,0:T(8,128)(2,1)} fusion(bf16[2,296,16,64]{1,3,2,0:T(8,128)(2,1)} %bitcast.139, f32[2,16,296,592]{3,2,1,0:T(8,128)} %fusion.113, f32[2,16,296]{2,1,0:T(8,128)S(1)} %log_add_fusion, f32[2,16,296,592]{3,2,1,0:T(8,128)} %get-tuple-element.73, pred[592]{0:T(1024)(128)(4,1)S(1)} %iota_compare_fusion), kind=kOutput, calls=%fused_computation.82 | convolution fusion | flops 780654400 | bytes 48535120 | tf_op jit(solution)/shard_map/ihcs,ichd->ishd/dot_general | solution.py:181
  654.4 6.5 copy.113
  660.9 3.9 copy.129
  666.2 4.8 bitcast_convert_fusion.3
  671.5 70.3 %bitcast_convert_fusion.4 = (bf16[2,296,16,64]{1,3,2,0:T(8,128)(2,1)S(1)}, f32[2,16,64,296]{3,2,1,0:T(8,128)}) fusion(bf16[2,592,16,64]{1,3,2,0:T(8,128)(2,1)} %bitcast.131, f32[2,16,296,592]{3,2,1,0:T(8,128)} %fusion.113, f32[2,16,296]{2,1,0:T(8,128)S(1)} %log_add_fusion, f32[2,16,296,592]{3,2,1,0:T(8,128)} %get-tuple-element.73, ...), kind=kOutput, calls=%fused_computation.42 | convolution fusion | flops 780048192 | bytes 50959952 | tf_op jit(solution)/shard_map/ihcs,ishd->ichd/dot_general | solution.py:178
  743.3 2.1 bitcast_reduce_fusion
  745.6 3.4 reshape.179
  750.3 4.3 reshape.177
  754.7 1.8 copy.114
  756.7 9.0 fusion.46
  768.9 12.0 %bitcast_convert_fusion.1 = bf16[1024,4096]{1,0:T(8,128)(2,1)} fusion(bf16[2,296,4096]{2,1,0:T(8,128)(2,1)} %copy-done.47, f32[2,296,1024]{2,1,0:T(8,128)} %copy-done.3, f32[1024]{0:T(1024)S(1)} %bitcast.167, f32[1024]{0:T(1024)S(1)} %bitcast.158, f32[2,296]{1,0:T(2,128)S(1)} %add_rsqrt_fusion, f32[2,296]{1,0:T(2,128)S(1)} %broadcast_multiply_fusion.4), kind=kOutput, calls=%fused_computation.9 | convolution fusion | flops 4973281280 | bytes 15676032 | tf_op jit(solution)/shard_map/icd,icf->df/dot_general | solution.py:159
  781.5 42.7 %reduce-scatter.47.cloned.1.call-done = bf16[64,2]{1,0:T(8,128)(2,1)} async-done(((bf16[1024,2]{1,0:T(8,128)(2,1)}), bf16[64,2]{1,0:T(8,128)(2,1)}) %reduce-scatter.47.cloned.1.call-update) | async-done | bytes 272
  824.3 9.2 bitcast_convert_fusion.2
  833.6 49.5 %reduce-scatter.51.cloned.1.call-done = bf16[64,10]{1,0:T(8,128)(2,1)} async-done(((bf16[1024,10]{1,0:T(8,128)(2,1)}), bf16[64,10]{1,0:T(8,128)(2,1)}) %reduce-scatter.51.cloned.1.call-update) | async-done | bytes 1296
  883.2 10.7 add_convert_fusion
  894.0 95.6 %reduce-scatter.35.cloned.1.call-done = bf16[64,4096]{1,0:T(8,128)(2,1)} async-done(((bf16[1024,4096]{1,0:T(8,128)(2,1)}), bf16[64,4096]{1,0:T(8,128)(2,1)}) %reduce-scatter.35.cloned.1.call-update) | async-done | bytes 524304 | tf_op jit(solution)/shard_map/reduce_scatter | solution.py:224
  989.7 12.0 %reduce-scatter.33.cloned.1.call-done = bf16[64,512]{1,0:T(8,128)(2,1)} async-done(((bf16[64,1024]{1,0:T(8,128)(2,1)}), bf16[64,512]{1,0:T(8,128)(2,1)}) %reduce-scatter.33.cloned.1.call-update) | async-done | bytes 65552 | tf_op jit(solution)/shard_map/reduce_scatter | solution.py:241
  1001.7 1.7 multiply_subtract_fusion.3
  1003.5 4.4 fusion.45
  1007.9 5.8 reduce-scatter.49.cloned.1.call-done
  1014.5 88.1 %reduce-scatter.27.cloned.1.call-done = bf16[64,3072]{1,0:T(8,128)(2,1)} async-done(((bf16[1024,3072]{1,0:T(8,128)(2,1)}), bf16[64,3072]{1,0:T(8,128)(2,1)}) %reduce-scatter.27.cloned.1.call-update) | async-done | bytes 393232 | tf_op jit(solution)/shard_map/reduce_scatter | solution.py:218
  1103.2 10.3 reduce-scatter.53.cloned.1.call-done
  1115.0 15.5 %reduce-scatter.37.cloned.1.call-done = bf16[64,2048]{1,0:T(8,128)(2,1)} async-done(((bf16[64,4096]{1,0:T(8,128)(2,1)}), bf16[64,2048]{1,0:T(8,128)(2,1)}) %reduce-scatter.37.cloned.1.call-update) | async-done | bytes 262160 | tf_op jit(solution)/shard_map/reduce_scatter | solution.py:244
  1130.5 2.4 multiply_subtract_fusion.1
  1132.8 12.9 %reduce-scatter.29.cloned.1.call-done = bf16[64,1536]{1,0:T(8,128)(2,1)} async-done(((bf16[64,3072]{1,0:T(8,128)(2,1)}), bf16[64,1536]{1,0:T(8,128)(2,1)}) %reduce-scatter.29.cloned.1.call-update) | async-done | bytes 196624 | tf_op jit(solution)/shard_map/reduce_scatter | solution.py:238
  1145.8 2.2 multiply_subtract_fusion.2
  (191 shorter events, 23.1 us)
Async XLA Ops:
  7.2 60.8 %copy-start = (bf16[2,296,1024]{2,1,0:T(8,128)(2,1)S(1)}, bf16[2,296,1024]{2,1,0:T(8,128)(2,1)}, u32[]{:S(2)}) copy-start(bf16[2,296,1024]{2,1,0:T(8,128)(2,1)} %param.20) | copy-start | bytes 3637252
  7.2 73.1 %all-gather.11.cloned.1.call-start = ((), (), s32[]{:S(2)}) async-start(), calls=%async_computation.14 | async-start | bytes 6684672 | tf_op jit(solution)/shard_map/all_gather | solution.py:79
  17.1 114.9 %all-gather.13.cloned.1.call-start = ((), (), s32[]{:S(2)}) async-start(), calls=%async_computation.15 | async-start | bytes 3637248 | tf_op jit(solution)/shard_map/all_gather | solution.py:104
  68.2 18.7 %copy-start.26 = (f32[2,296]{1,0:T(2,128)}, f32[2,296]{1,0:T(2,128)S(1)}, u32[]{:S(2)}) copy-start(f32[2,296]{1,0:T(2,128)S(1)} %broadcast_multiply_fusion.5) | copy-start | bytes 7108
  68.7 18.2 %copy-start.30 = (f32[2,296]{1,0:T(2,128)}, f32[2,296]{1,0:T(2,128)S(1)}, u32[]{:S(2)}) copy-start(f32[2,296]{1,0:T(2,128)S(1)} %add_rsqrt_fusion.1) | copy-start | bytes 7108
  68.8 18.2 %copy-start.28 = (f32[1,1024]{1,0:T(1,128)}, f32[1,1024]{1,0:T(1,128)S(1)}, u32[]{:S(2)}) copy-start(f32[1,1024]{1,0:T(1,128)S(1)} %get-tuple-element.71) | copy-start | bytes 12292
  69.4 17.6 %copy-start.37 = (f32[1,1024]{1,0:T(1,128)}, f32[1,1024]{1,0:T(1,128)S(1)}, u32[]{:S(2)}) copy-start(f32[1,1024]{1,0:T(1,128)S(1)} %get-tuple-element.69) | copy-start | bytes 12292
  69.4 219.5 %copy-start.39 = (f32[1,1024]{1,0:T(1,128)}, f32[1,1024]{1,0:T(1,128)S(1)}, u32[]{:S(2)}) copy-start(f32[1,1024]{1,0:T(1,128)S(1)} %get-tuple-element.65) | copy-start | bytes 12292
  87.0 3.7 copy-start.6
  90.7 3.2 copy-start.17
  90.7 8.3 copy-start.7
  90.7 79.6 %all-gather.15.cloned.1.call-start = ((), (), s32[]{:S(2)}) async-start(), calls=%async_computation.16 | async-start | bytes 3637248 | tf_op jit(solution)/shard_map/all_gather | solution.py:103
  93.8 120.0 %all-gather.17.cloned.1.call-start = ((), (), s32[]{:S(2)}) async-start(), calls=%async_computation.17 | async-start | bytes 2228224 | tf_op jit(solution)/shard_map/all_gather | solution.py:80
  99.0 189.9 %all-gather.19.cloned.1.call-start = ((), (), s32[]{:S(2)}) async-start(), calls=%async_computation.18 | async-start | bytes 8912896 | tf_op jit(solution)/shard_map/all_gather | solution.py:81
  114.0 300.8 %reduce-scatter.39.cloned.1.call-start = ((), (), s32[]{:S(2)}) async-start(), calls=%async_computation.26 | async-start | bytes 8912896 | tf_op jit(solution)/shard_map/reduce_scatter | solution.py:227
  114.4 186.8 %copy-start.32 = (f32[296]{0:T(512)}, f32[296]{0:T(512)S(1)}, u32[]{:S(2)}) copy-start(f32[296]{0:T(512)S(1)} %fusion.82) | copy-start | bytes 3556
  116.3 58.4 %copy-start.5 = (bf16[2,296,1024]{1,2,0:T(8,128)(2,1)}, bf16[2,296,1024]{1,2,0:T(8,128)(2,1)S(1)}, u32[]{:S(2)}) copy-start(bf16[2,296,1024]{1,2,0:T(8,128)(2,1)S(1)} %copy.103) | copy-start | bytes 3637252
  188.9 9.5 copy-start.1
  209.1 8.0 copy-start.45
  288.9 14.5 %copy-start.13 = (bf16[2,296,1024]{2,1,0:T(8,128)(2,1)S(1)}, bf16[2,296,1024]{2,1,0:T(8,128)(2,1)}, u32[]{:S(2)}) copy-start(bf16[2,296,1024]{2,1,0:T(8,128)(2,1)} %param.21) | copy-start | bytes 3637252
  301.2 2.2 copy-start.48
  312.6 118.8 %copy-start.19 = (f32[256,512]{1,0:T(8,128)S(1)}, f32[256,512]{1,0:T(8,128)}, u32[]{:S(2)}) copy-start(f32[256,512]{1,0:T(8,128)} %param.25) | copy-start | bytes 1572868
  312.6 118.8 %copy-start.20 = (f32[256,512]{1,0:T(8,128)S(1)}, f32[256,512]{1,0:T(8,128)}, u32[]{:S(2)}) copy-start(f32[256,512]{1,0:T(8,128)} %param.31) | copy-start | bytes 1572868
  312.6 118.8 %reduce-scatter.41.cloned.1.call-start = ((), (), s32[]{:S(2)}) async-start(), calls=%async_computation.27 | async-start | bytes 786432 | tf_op jit(solution)/shard_map/reduce_scatter | solution.py:247
  414.8 102.2 %all-gather.21.cloned.1.call-start = ((), (), s32[]{:S(2)}) async-start(), calls=%async_computation.19 | async-start | bytes 8912896 | tf_op jit(solution)/shard_map/all_gather | solution.py:82
  442.6 303.0 %reduce-scatter.45.cloned.1.call-start = ((), (), s32[]{:S(2)}) async-start(), calls=%async_computation.29 | async-start | bytes 3637248
  517.1 12.6 %copy-start.4 = (f32[2,296,1024]{2,1,0:T(8,128)S(1)}, f32[2,296,1024]{2,1,0:T(8,128)}, u32[]{:S(2)}) copy-start(f32[2,296,1024]{2,1,0:T(8,128)} %copy-done.3) | copy-start | bytes 7274500
  529.7 10.4 copy-start.47
  529.7 10.4 copy-start.33
  540.1 2.7 copy-start.44
  569.5 180.8 %reduce-scatter.43.cloned.1.call-start = ((), (), s32[]{:S(2)}) async-start(), calls=%async_computation.28 | async-start | bytes 3637248
  664.8 116.2 %reduce-scatter.31.cloned.1.call-start = ((), (), s32[]{:S(2)}) async-start(), calls=%async_computation.22 | async-start | bytes 2228224 | tf_op jit(solution)/shard_map/reduce_scatter | solution.py:221
  671.1 153.1 %reduce-scatter.47.cloned.1.call-start = ((), (), s32[]{:S(2)}) async-start(), calls=%async_computation.30 | async-start | bytes 278528
  750.3 6.1 copy-start.27
  750.3 6.1 copy-start.29
  750.3 6.1 copy-start.31
  756.7 9.0 copy-start.12
  756.7 12.2 %copy-start.40 = (f32[1,1024]{1,0:T(1,128)S(1)}, f32[1,1024]{1,0:T(1,128)}, u32[]{:S(2)}) copy-start(f32[1,1024]{1,0:T(1,128)} %copy-done.39) | copy-start | bytes 12292
  766.7 116.5 %reduce-scatter.51.cloned.1.call-start = ((), (), s32[]{:S(2)}) async-start(), calls=%async_computation.32 | async-start | bytes 278528
  768.8 220.8 %reduce-scatter.35.cloned.1.call-start = ((), (), s32[]{:S(2)}) async-start(), calls=%async_computation.24 | async-start | bytes 8912896 | tf_op jit(solution)/shard_map/reduce_scatter | solution.py:224
  780.9 43.4 %copy-start.11 = (bf16[2,296,1024]{2,1,0:T(8,128)(2,1)S(1)}, bf16[2,296,1024]{2,1,0:T(8,128)(2,1)}, u32[]{:S(2)}) copy-start(bf16[2,296,1024]{2,1,0:T(8,128)(2,1)} %copy.116) | copy-start | bytes 3637252
  780.9 43.4 %copy-start.38 = (f32[1,1024]{1,0:T(1,128)S(1)}, f32[1,1024]{1,0:T(1,128)}, u32[]{:S(2)}) copy-start(f32[1,1024]{1,0:T(1,128)} %copy-done.37) | copy-start | bytes 12292
  780.9 220.8 %reduce-scatter.33.cloned.1.call-start = ((), (), s32[]{:S(2)}) async-start(), calls=%async_computation.23 | async-start | bytes 196608 | tf_op jit(solution)/shard_map/reduce_scatter | solution.py:241
  781.5 232.2 %reduce-scatter.49.cloned.1.call-start = ((), (), s32[]{:S(2)}) async-start(), calls=%async_computation.31 | async-start | bytes 24576
  824.2 278.3 %reduce-scatter.27.cloned.1.call-start = ((), (), s32[]{:S(2)}) async-start(), calls=%async_computation.20 | async-start | bytes 6684672 | tf_op jit(solution)/shard_map/reduce_scatter | solution.py:218
  833.5 49.6 %copy-start.36 = (f32[1,1024]{1,0:T(1,128)S(1)}, f32[1,1024]{1,0:T(1,128)}, u32[]{:S(2)}) copy-start(f32[1,1024]{1,0:T(1,128)} %get-tuple-element.64) | copy-start | bytes 12292
  833.6 280.0 %reduce-scatter.53.cloned.1.call-start = ((), (), s32[]{:S(2)}) async-start(), calls=%async_computation.33 | async-start | bytes 24576
  883.1 247.3 %reduce-scatter.37.cloned.1.call-start = ((), (), s32[]{:S(2)}) async-start(), calls=%async_computation.25 | async-start | bytes 786432 | tf_op jit(solution)/shard_map/reduce_scatter | solution.py:244
  883.2 118.5 %copy-start.18 = (f32[64,512]{1,0:T(8,128)S(1)}, f32[64,512]{1,0:T(8,128)}, u32[]{:S(2)}) copy-start(f32[64,512]{1,0:T(8,128)} %param.23) | copy-start | bytes 393220
  883.2 118.5 %copy-start.23 = (f32[64,512]{1,0:T(8,128)S(1)}, f32[64,512]{1,0:T(8,128)}, u32[]{:S(2)}) copy-start(f32[64,512]{1,0:T(8,128)} %param.29) | copy-start | bytes 393220
  883.2 118.5 %copy-start.24 = (f32[64,512]{1,0:T(8,128)S(1)}, f32[64,512]{1,0:T(8,128)}, u32[]{:S(2)}) copy-start(f32[64,512]{1,0:T(8,128)} %param.35) | copy-start | bytes 393220
  989.6 156.1 %reduce-scatter.29.cloned.1.call-start = ((), (), s32[]{:S(2)}) async-start(), calls=%async_computation.21 | async-start | bytes 589824 | tf_op jit(solution)/shard_map/reduce_scatter | solution.py:238
  1003.4 99.2 %copy-start.41 = (f32[2,32]{1,0:T(2,128)S(1)}, f32[2,32]{1,0:T(2,128)}, u32[]{:S(2)}) copy-start(f32[2,32]{1,0:T(2,128)} %param.26) | copy-start | bytes 772
  1003.4 99.3 %copy-start.42 = (f32[2,32]{1,0:T(2,128)S(1)}, f32[2,32]{1,0:T(2,128)}, u32[]{:S(2)}) copy-start(f32[2,32]{1,0:T(2,128)} %param.32) | copy-start | bytes 772
  1003.4 99.3 %copy-start.43 = (f32[2,32]{1,0:T(2,128)S(1)}, f32[2,32]{1,0:T(2,128)}, u32[]{:S(2)}) copy-start(f32[2,32]{1,0:T(2,128)} %param.38) | copy-start | bytes 772
  1003.4 110.9 %copy-start.25 = (f32[10,32]{1,0:T(8,128)S(1)}, f32[10,32]{1,0:T(8,128)}, u32[]{:S(2)}) copy-start(f32[10,32]{1,0:T(8,128)} %param.27) | copy-start | bytes 3844
  1003.4 110.9 %copy-start.34 = (f32[10,32]{1,0:T(8,128)S(1)}, f32[10,32]{1,0:T(8,128)}, u32[]{:S(2)}) copy-start(f32[10,32]{1,0:T(8,128)} %param.33) | copy-start | bytes 3844
  1003.4 110.9 %copy-start.35 = (f32[10,32]{1,0:T(8,128)S(1)}, f32[10,32]{1,0:T(8,128)}, u32[]{:S(2)}) copy-start(f32[10,32]{1,0:T(8,128)} %param.39) | copy-start | bytes 3844
  1003.4 127.0 %copy-start.8 = (f32[64,2048]{1,0:T(8,128)S(1)}, f32[64,2048]{1,0:T(8,128)}, u32[]{:S(2)}) copy-start(f32[64,2048]{1,0:T(8,128)} %param.24) | copy-start | bytes 1572868
  1003.4 127.0 %copy-start.15 = (f32[64,2048]{1,0:T(8,128)S(1)}, f32[64,2048]{1,0:T(8,128)}, u32[]{:S(2)}) copy-start(f32[64,2048]{1,0:T(8,128)} %param.30) | copy-start | bytes 1572868
  1003.4 127.0 %copy-start.16 = (f32[64,2048]{1,0:T(8,128)S(1)}, f32[64,2048]{1,0:T(8,128)}, u32[]{:S(2)}) copy-start(f32[64,2048]{1,0:T(8,128)} %param.36) | copy-start | bytes 1572868
  1007.9 137.9 %copy-start.9 = (f32[64,1536]{1,0:T(8,128)S(1)}, f32[64,1536]{1,0:T(8,128)}, u32[]{:S(2)}) copy-start(f32[64,1536]{1,0:T(8,128)} %param.22) | copy-start | bytes 1179652
  1007.9 137.9 %copy-start.21 = (f32[64,1536]{1,0:T(8,128)S(1)}, f32[64,1536]{1,0:T(8,128)}, u32[]{:S(2)}) copy-start(f32[64,1536]{1,0:T(8,128)} %param.28) | copy-start | bytes 1179652
  1007.9 137.9 %copy-start.22 = (f32[64,1536]{1,0:T(8,128)S(1)}, f32[64,1536]{1,0:T(8,128)}, u32[]{:S(2)}) copy-start(f32[64,1536]{1,0:T(8,128)} %param.34) | copy-start | bytes 1179652
  (5 other events, 8.2 us)
Sparse Core Ops, SparseCore 0:
  17.2 63.0 all-gather.10
  90.9 41.0 all-gather.12
  133.5 36.7 all-gather.14
  172.4 41.4 all-gather.16
  215.8 73.0 all-gather.18
  312.7 102.0 reduce-scatter.38
  417.1 14.2 reduce-scatter.40
  442.7 74.2 all-gather.20
  569.7 34.1 reduce-scatter.44
  664.9 34.8 reduce-scatter.42
  703.6 61.9 reduce-scatter.30
  769.5 54.6 reduce-scatter.46
  828.3 54.7 reduce-scatter.50
  887.0 102.5 reduce-scatter.34
  991.6 9.9 reduce-scatter.32
  1003.7 9.9 reduce-scatter.48
  1017.5 85.0 reduce-scatter.26
  1104.6 8.8 reduce-scatter.52
  1115.8 14.6 reduce-scatter.36
  1132.5 13.1 reduce-scatter.28
where the time goes:
time: 1160 us; the launch traced here: 1150 us
  waiting for transfers between devices  661 us (57%)
  matrix products  294 us (25%)
  blocking collectives  86.4 us (7%)
  local copies, waits for them, and re-layouts  61.1 us (5%)
  other arithmetic  34.6 us (3%)
  between operations  15.3 us (1%)
    unnamed x26, waiting for transfers between devices  109 us
    reduce_scatter x1, waiting for transfers between devices, body(): lax.psum_scatter(g_down.astype(jnp.bfloat16), 'dp', scatter_dimension=0,...  102 us
    reduce_scatter x1, waiting for transfers between devices, body(): lax.psum_scatter(g_up.astype(jnp.bfloat16), 'dp', scatter_dimension=0, ti...  95.6 us
    reduce_scatter x1, waiting for transfers between devices, body(): lax.psum_scatter(g_qkv.astype(jnp.bfloat16), 'dp', scatter_dimension=0, t...  88.1 us
    all_gather x1, waiting for transfers between devices, body(): lax.all_gather(block_parts[3], 'dp', axis=0, tiled=True)  74.4 us
    dot_general x1, matrix products, body(): jnp.einsum('ihcs,ichd->ishd', grad_scores, query_heads, preferred_element...  70.8 us
    dot_general x1, matrix products, body(): jnp.einsum('ihcs,ishd->ichd', grad_scores, key_heads, preferred_element_t...  70.3 us
    all_gather x1, waiting for transfers between devices, body(): lax.all_gather(block_parts[2], 'dp', axis=0, tiled=True)  69.8 us
  transfers between devices with their start and end apart: 20, of which 17 were waited for; matrix products, arithmetic and copies ran while one was open for 26% of the time, Pallas kernels for 0%

commit v1 on v0

--- a/solution.py
+++ b/solution.py
@@ -6,6 +6,27 @@
 HEAD_DIM = 64
 PATCH_TOK = 577
 STEP = 5
+
+
+def raise_sector(work_x, ndim_at):
+    f_now, y1, out_arr = (lax.axis_size("dp"), lax.axis_index("dp"), work_x.shape[ndim_at])
+    xs_all = []
+    for p, h in enumerate(work_x.shape):
+        xs_all.append(h * f_now if p == ndim_at else h)
+    y = lax.dynamic_update_slice_in_dim(
+        jnp.zeros(xs_all, work_x.dtype), work_x, y1 * out_arr, axis=ndim_at
+    )
+    d = 1
+    while d < f_now:
+        by_place = []
+        p = 0
+        while p < f_now:
+            by_place.append((p, (p + 1) % f_now))
+            p += 1
+        work_x = lax.ppermute(work_x, axis_name="dp", perm=by_place)
+        y = lax.dynamic_update_slice_in_dim(y, work_x, (y1 - d) % f_now * out_arr, axis=ndim_at)
+        d += 1
+    return y
 
 
 def normalize(rows):
@@ -78,7 +99,7 @@
     wide_qkv, wide_out, wide_up, wide_down, wide_gains, wide_biases = (
         lax.all_gather(block_parts[0], "dp", axis=0, tiled=True),
         lax.all_gather(block_parts[1], "dp", axis=0, tiled=True),
-        lax.all_gather(block_parts[2], "dp", axis=0, tiled=True),
+        raise_sector(block_parts[2], ndim_at=0),
         lax.all_gather(block_parts[3], "dp", axis=0, tiled=True),
         lax.all_gather(block_parts[4], "dp", axis=1, tiled=True),
         lax.all_gather(block_parts[5], "dp", axis=1, tiled=True),

time: 1160 us -> 1200 us (1.034)
  waiting for transfers between devices: 661 us -> 685 us
  local copies, waits for them, and re-layouts: 61.1 us -> 78.7 us
    ppermute x0 -> x15, waiting for transfers between devices: none -> 149 us  [raise_sector(): work_x = lax.ppermute(work_x, axis_name='dp', perm=by_place)]
    all_gather x1 -> x0, waiting for transfers between devices: 69.8 us -> none  [body(): lax.all_gather(block_parts[2], 'dp', axis=0, tiled=True)]
    all_gather x1, waiting for transfers between devices: 33.9 us -> 0.01 us  [body(): lax.all_gather(keys, 'seq', axis=1, tiled=True)]
    all_gather x1, waiting for transfers between devices: 15.7 us -> 0.02 us  [body(): lax.all_gather(values, 'seq', axis=1, tiled=True)]
    dynamic_update_slice x0 -> x16, local copies, waits for them, and re-layouts: none -> 14.4 us  [the longest x15 13.6 us: raise_sector(): lax.dynamic_update_slice_in_dim(y, work_x, (y1 - d) % f_now * out_arr, ax...]
    unnamed x114 -> x122, local copies, waits for them, and re-layouts: 43.1 us -> 41.6 us
    unnamed x26 -> x25, waiting for transfers between devices: 109 us -> 110 us
  transfers between devices with their start and end apart: 20 -> 34, of which waited for: 17 -> 28; matrix products, arithmetic and copies ran while one was open for 26% -> 26% of each run, Pallas kernels for 0% -> 0%
where the time goes in v1:
time: 1200 us; the launch traced here: 1190 us
  waiting for transfers between devices  685 us (57%)
  matrix products  295 us (25%)
  blocking collectives  81.7 us (7%)
  local copies, waits for them, and re-layouts  78.7 us (7%)
  other arithmetic  36 us (3%)
  between operations  15.5 us (1%)
    ppermute x15, waiting for transfers between devices, raise_sector(): work_x = lax.ppermute(work_x, axis_name='dp', perm=by_place)  149 us
    unnamed x25, waiting for transfers between devices  110 us
    reduce_scatter x1, waiting for transfers between devices, body(): lax.psum_scatter(g_down.astype(jnp.bfloat16), 'dp', scatter_dimension=0,...  102 us
    reduce_scatter x1, waiting for transfers between devices, body(): lax.psum_scatter(g_up.astype(jnp.bfloat16), 'dp', scatter_dimension=0, ti...  95.8 us
    reduce_scatter x1, waiting for transfers between devices, body(): lax.psum_scatter(g_qkv.astype(jnp.bfloat16), 'dp', scatter_dimension=0, t...  88.1 us
    all_gather x1, waiting for transfers between devices, body(): lax.all_gather(block_parts[3], 'dp', axis=0, tiled=True)  74.4 us
    dot_general x1, matrix products, body(): jnp.einsum('ihcs,ichd->ishd', grad_scores, query_heads, preferred_element...  70.8 us
    dot_general x1, matrix products, body(): jnp.einsum('ihcs,ishd->ichd', grad_scores, key_heads, preferred_element_t...  70.2 us
  transfers between devices with their start and end apart: 34, of which 28 were waited for; matrix products, arithmetic and copies ran while one was open for 26% of the time, Pallas kernels for 0%

profile of v1, /device:TPU:0, one launch (start us, length us, event | category | flops | bytes accessed | tf_op | source)
XLA Modules:
  0.0 1194.2 jit_solution(18324822050004535026)
XLA Ops:
  8.4 8.7 all_gather.43
  17.8 4.3 all-gather.2
  22.2 22.7 %all-gather.3 = bf16[16,64,10]{1,2,0:T(8,128)(2,1)S(1)} all-gather(bf16[1,64,10]{1,2,0:T(8,128)(2,1)S(1)} %reshape.162), channel_id=1, replica_groups=mesh['dp'=16,'seq'=2] {'dp'}, dimensions={0}, use_global_device_ids=true | all-gather | bytes 21760 | tf_op jit(solution)/shard_map/all_gather | solution.py:105
  45.7 4.2 all-gather
  50.0 17.9 %all-gather.1 = bf16[16,64,2]{1,2,0:T(2,128)(2,1)S(1)} all-gather(bf16[1,64,2]{1,2,0:T(2,128)(2,1)S(1)} %reshape.158), channel_id=1, replica_groups=mesh['dp'=16,'seq'=2] {'dp'}, dimensions={0}, use_global_device_ids=true | all-gather | bytes 4352 | tf_op jit(solution)/shard_map/all_gather | solution.py:104
  70.8 9.5 all-gather.10.cloned.1.call-done
  80.3 6.6 fusion.31
  90.8 9.8 all_gather.49
  100.6 11.3 collective-permute-done
  114.9 8.3 collective-permute-done.1
  123.2 11.3 collective-permute-done.2
  135.3 10.5 collective-permute-done.3
  145.8 11.3 collective-permute-done.4
  157.9 10.6 collective-permute-done.5
  168.5 5.5 all_gather.47
  174.5 5.5 collective-permute-done.6
  180.0 4.3 broadcast_in_dim.20
  185.2 9.5 collective-permute-done.7
  196.4 9.8 collective-permute-done.8
  207.8 13.5 %collective-permute-done.9 = bf16[64,4096]{1,0:T(8,128)(2,1)S(1)} collective-permute-done((bf16[64,4096]{1,0:T(8,128)(2,1)S(1)}, bf16[64,4096]{1,0:T(8,128)(2,1)S(1)}, u32[]{:S(2)}, u32[]{:S(2)}) %collective-permute-start.9) | collective-permute-done | bytes 524320 | tf_op jit(solution)/shard_map/ppermute | solution.py:26
  224.0 8.6 collective-permute-done.10
  234.2 9.7 collective-permute-done.11
  245.6 9.6 collective-permute-done.12
  256.9 9.6 collective-permute-done.13
  268.7 9.6 collective-permute-done.14
  281.0 4.9 copy.102
  285.9 4.4 copy.104
  290.2 14.1 %fusion.2 = (f32[2,16,296]{2,1,0:T(8,128)S(1)}, f32[2,16,296,592]{3,2,1,0:T(8,128)}) fusion(pred[592]{0:T(1024)(128)(4,1)S(1)} %iota_compare_fusion, bf16[2,296,16,64]{1,3,2,0:T(8,128)(2,1)S(1)} %bitcast.138, bf16[2,592,16,64]{1,3,2,0:T(8,128)(2,1)} %bitcast.130), kind=kOutput, calls=%fused_computation.7 | convolution fusion | flops 734563072 | bytes 26105424 | tf_op jit(solution)/shard_map/ichd,ishd->ihcs/dot_general | solution.py:133
  304.4 9.4 exponential_reduce_fusion
  313.8 10.7 convolution_convert_fusion.1
  324.6 3.8 fusion.109
  328.8 11.7 multiply_convert_fusion.1
  342.8 9.2 bitcast_convert_fusion
  352.0 101.6 %reduce-scatter.39.cloned.1.call-done = bf16[256,1024]{1,0:T(8,128)(2,1)} async-done(((bf16[4096,1024]{1,0:T(8,128)(2,1)}), bf16[256,1024]{1,0:T(8,128)(2,1)}) %reduce-scatter.39.cloned.1.call-update) | async-done | bytes 524304 | tf_op jit(solution)/shard_map/reduce_scatter | solution.py:248
  453.7 16.3 %reduce-scatter.41.cloned.1.call-done = bf16[256,512]{1,0:T(8,128)(2,1)} async-done(((bf16[256,1024]{1,0:T(8,128)(2,1)}), bf16[256,512]{1,0:T(8,128)(2,1)}) %reduce-scatter.41.cloned.1.call-update) | async-done | bytes 262160 | tf_op jit(solution)/shard_map/reduce_scatter | solution.py:268
  472.6 8.7 all_gather.50
  481.3 74.4 %all-gather.18.cloned.1.call-done = bf16[4096,1024]{1,0:T(8,128)(2,1)} async-done(((bf16[256,1024]{1,0:T(8,128)(2,1)}), bf16[4096,1024]{1,0:T(8,128)(2,1)}) %all-gather.18.cloned.1.call-update) | async-done | bytes 8388624 | tf_op jit(solution)/shard_map/all_gather | solution.py:103
  555.7 12.6 %fusion.112 = (bf16[4096]{0:T(1024)(128)(2,1)S(1)}, bf16[2,296,4096]{2,1,0:T(8,128)(2,1)S(1)}) fusion(f32[2,296,4096]{2,1,0:T(8,128)} %get-tuple-element.77, f32[4096]{0:T(1024)S(1)} %bitcast.160, bf16[4096,1024]{1,0:T(8,128)(2,1)} %all-gather.18.cloned.1.call-done, bf16[2,296,1024]{2,1,0:T(8,128)(2,1)S(1)} %copy-done.12, f32[296]{0:T(512)} %copy-done.36), kind=kOutput, calls=%fused_computation.164 | convolution fusion | flops 4996968448 | bytes 24175776 | tf_op jit(solution)/shard_map/icd,fd->icf/dot_general | solution.py:176
  568.4 10.3 multiply_reduce_fusion.1
  585.8 12.0 %convolution_convert_fusion = bf16[2,16,64,592]{3,2,1,0:T(8,128)(2,1)} fusion(bf16[2,296,16,64]{1,3,2,0:T(8,128)(2,1)S(1)} %bitcast.136, f32[2,16,296]{2,1,0:T(8,128)S(1)} %log_add_fusion, f32[2,16,296,592]{3,2,1,0:T(8,128)} %get-tuple-element.73, pred[592]{0:T(1024)(128)(4,1)S(1)} %iota_compare_fusion), kind=kOutput, calls=%fused_computation.83 | convolution fusion | flops 741392384 | bytes 26105424 | tf_op jit(solution)/shard_map/ihcs,ichd->ishd/dot_general | solution.py:194
  597.8 6.5 copy.115
  604.3 3.9 copy.130
  608.7 13.8 %fusion.113 = f32[2,16,296,592]{3,2,1,0:T(8,128)} fusion(bf16[2,296,16,64]{1,3,2,0:T(8,128)(2,1)S(1)} %bitcast.137, bf16[2,592,16,64]{1,3,2,0:T(8,128)(2,1)} %bitcast.128), kind=kOutput, calls=%fused_computation.165 | convolution fusion | flops 717750272 | bytes 26066944 | tf_op jit(solution)/shard_map/ichd,ishd->ihcs/dot_general | solution.py:191
  622.5 70.8 %fusion.59 = bf16[2,16,64,592]{3,2,1,0:T(8,128)(2,1)} fusion(bf16[2,296,16,64]{1,3,2,0:T(8,128)(2,1)} %bitcast.139, f32[2,16,296,592]{3,2,1,0:T(8,128)} %fusion.113, f32[2,16,296]{2,1,0:T(8,128)S(1)} %log_add_fusion, f32[2,16,296,592]{3,2,1,0:T(8,128)} %get-tuple-element.73, pred[592]{0:T(1024)(128)(4,1)S(1)} %iota_compare_fusion), kind=kOutput, calls=%fused_computation.82 | convolution fusion | flops 780654400 | bytes 48535120 | tf_op jit(solution)/shard_map/ihcs,ichd->ishd/dot_general | solution.py:202
  693.3 6.5 copy.113
  699.8 4.0 copy.129
  703.9 4.8 bitcast_convert_fusion.3
  709.0 70.2 %bitcast_convert_fusion.4 = (bf16[2,296,16,64]{1,3,2,0:T(8,128)(2,1)S(1)}, f32[2,16,64,296]{3,2,1,0:T(8,128)}) fusion(bf16[2,592,16,64]{1,3,2,0:T(8,128)(2,1)} %bitcast.131, f32[2,16,296,592]{3,2,1,0:T(8,128)} %fusion.113, f32[2,16,296]{2,1,0:T(8,128)S(1)} %log_add_fusion, f32[2,16,296,592]{3,2,1,0:T(8,128)} %get-tuple-element.73, ...), kind=kOutput, calls=%fused_computation.42 | convolution fusion | flops 780048192 | bytes 50959952 | tf_op jit(solution)/shard_map/ihcs,ishd->ichd/dot_general | solution.py:199
  783.1 3.4 reshape.179
  787.8 4.3 reshape.177
  793.8 9.8 fusion.46
  806.8 12.0 %bitcast_convert_fusion.1 = bf16[1024,4096]{1,0:T(8,128)(2,1)} fusion(bf16[2,296,4096]{2,1,0:T(8,128)(2,1)} %copy-done.51, f32[2,296,1024]{2,1,0:T(8,128)} %copy-done.3, f32[1024]{0:T(1024)S(1)} %bitcast.167, f32[1024]{0:T(1024)S(1)} %bitcast.158, f32[2,296]{1,0:T(2,128)S(1)} %add_rsqrt_fusion, f32[2,296]{1,0:T(2,128)S(1)} %broadcast_multiply_fusion.4), kind=kOutput, calls=%fused_computation.9 | convolution fusion | flops 4973281280 | bytes 15676032 | tf_op jit(solution)/shard_map/icd,icf->df/dot_general | solution.py:180
  819.4 44.0 %reduce-scatter.47.cloned.1.call-done = bf16[64,2]{1,0:T(8,128)(2,1)} async-done(((bf16[1024,2]{1,0:T(8,128)(2,1)}), bf16[64,2]{1,0:T(8,128)(2,1)}) %reduce-scatter.47.cloned.1.call-update) | async-done | bytes 272
  863.5 9.2 bitcast_convert_fusion.2
  872.8 49.3 %reduce-scatter.51.cloned.1.call-done = bf16[64,10]{1,0:T(8,128)(2,1)} async-done(((bf16[1024,10]{1,0:T(8,128)(2,1)}), bf16[64,10]{1,0:T(8,128)(2,1)}) %reduce-scatter.51.cloned.1.call-update) | async-done | bytes 1296
  922.3 10.7 add_convert_fusion
  933.0 95.8 %reduce-scatter.35.cloned.1.call-done = bf16[64,4096]{1,0:T(8,128)(2,1)} async-done(((bf16[1024,4096]{1,0:T(8,128)(2,1)}), bf16[64,4096]{1,0:T(8,128)(2,1)}) %reduce-scatter.35.cloned.1.call-update) | async-done | bytes 524304 | tf_op jit(solution)/shard_map/reduce_scatter | solution.py:245
  1028.9 12.0 %reduce-scatter.33.cloned.1.call-done = bf16[64,512]{1,0:T(8,128)(2,1)} async-done(((bf16[64,1024]{1,0:T(8,128)(2,1)}), bf16[64,512]{1,0:T(8,128)(2,1)}) %reduce-scatter.33.cloned.1.call-update) | async-done | bytes 65552 | tf_op jit(solution)/shard_map/reduce_scatter | solution.py:262
  1042.7 4.4 fusion.45
  1047.1 5.8 reduce-scatter.49.cloned.1.call-done
  1053.7 88.1 %reduce-scatter.27.cloned.1.call-done = bf16[64,3072]{1,0:T(8,128)(2,1)} async-done(((bf16[1024,3072]{1,0:T(8,128)(2,1)}), bf16[64,3072]{1,0:T(8,128)(2,1)}) %reduce-scatter.27.cloned.1.call-update) | async-done | bytes 393232 | tf_op jit(solution)/shard_map/reduce_scatter | solution.py:239
  1142.5 10.5 reduce-scatter.53.cloned.1.call-done
  1154.4 15.3 %reduce-scatter.37.cloned.1.call-done = bf16[64,2048]{1,0:T(8,128)(2,1)} async-done(((bf16[64,4096]{1,0:T(8,128)(2,1)}), bf16[64,2048]{1,0:T(8,128)(2,1)}) %reduce-scatter.37.cloned.1.call-update) | async-done | bytes 262160 | tf_op jit(solution)/shard_map/reduce_scatter | solution.py:265
  1172.1 13.1 %reduce-scatter.29.cloned.1.call-done = bf16[64,1536]{1,0:T(8,128)(2,1)} async-done(((bf16[64,3072]{1,0:T(8,128)(2,1)}), bf16[64,1536]{1,0:T(8,128)(2,1)}) %reduce-scatter.29.cloned.1.call-update) | async-done | bytes 196624 | tf_op jit(solution)/shard_map/reduce_scatter | solution.py:259
  (243 shorter events, 64.0 us)
Async XLA Ops:
  7.2 62.4 %copy-start = (bf16[2,296,1024]{2,1,0:T(8,128)(2,1)S(1)}, bf16[2,296,1024]{2,1,0:T(8,128)(2,1)}, u32[]{:S(2)}) copy-start(bf16[2,296,1024]{2,1,0:T(8,128)(2,1)} %param.20) | copy-start | bytes 3637252
  7.2 73.1 %all-gather.10.cloned.1.call-start = ((), (), s32[]{:S(2)}) async-start(), calls=%async_computation.14 | async-start | bytes 6684672 | tf_op jit(solution)/shard_map/all_gather | solution.py:100
  17.1 264.0 %all-gather.12.cloned.1.call-start = ((), (), s32[]{:S(2)}) async-start(), calls=%async_computation.15 | async-start | bytes 3637248 | tf_op jit(solution)/shard_map/all_gather | solution.py:125
  69.6 17.3 %copy-start.30 = (f32[2,296]{1,0:T(2,128)}, f32[2,296]{1,0:T(2,128)S(1)}, u32[]{:S(2)}) copy-start(f32[2,296]{1,0:T(2,128)S(1)} %broadcast_multiply_fusion.5) | copy-start | bytes 7108
  70.1 16.8 %copy-start.34 = (f32[2,296]{1,0:T(2,128)}, f32[2,296]{1,0:T(2,128)S(1)}, u32[]{:S(2)}) copy-start(f32[2,296]{1,0:T(2,128)S(1)} %add_rsqrt_fusion.1) | copy-start | bytes 7108
  70.1 16.8 %copy-start.32 = (f32[1,1024]{1,0:T(1,128)}, f32[1,1024]{1,0:T(1,128)S(1)}, u32[]{:S(2)}) copy-start(f32[1,1024]{1,0:T(1,128)S(1)} %get-tuple-element.71) | copy-start | bytes 12292
  90.7 77.8 %copy-start.15 = (f32[64,512]{1,0:T(8,128)S(1)}, f32[64,512]{1,0:T(8,128)}, u32[]{:S(2)}) copy-start(f32[64,512]{1,0:T(8,128)} %param.23) | copy-start | bytes 393220
  90.7 195.2 %all-gather.14.cloned.1.call-start = ((), (), s32[]{:S(2)}) async-start(), calls=%async_computation.16 | async-start | bytes 3637248 | tf_op jit(solution)/shard_map/all_gather | solution.py:124
  100.6 11.3 collective-permute-start
  111.9 11.3 collective-permute-start.1
  114.8 209.7 %all-gather.16.cloned.1.call-start = ((), (), s32[]{:S(2)}) async-start(), calls=%async_computation.17 | async-start | bytes 2228224 | tf_op jit(solution)/shard_map/all_gather | solution.py:101
  123.2 11.3 collective-permute-start.2
  134.5 11.3 collective-permute-start.3
  145.8 22.7 %copy-start.21 = (bf16[64,4096]{1,0:T(8,128)(2,1)}, bf16[64,4096]{1,0:T(8,128)(2,1)S(1)}, u32[]{:S(2)}) copy-start(bf16[64,4096]{1,0:T(8,128)(2,1)S(1)} %collective-permute-done.3) | copy-start | bytes 1572868
  145.8 11.3 collective-permute-start.4
  157.1 11.4 collective-permute-start.5
  168.5 11.5 collective-permute-start.6
  174.1 279.5 %reduce-scatter.39.cloned.1.call-start = ((), (), s32[]{:S(2)}) async-start(), calls=%async_computation.25 | async-start | bytes 8912896 | tf_op jit(solution)/shard_map/reduce_scatter | solution.py:248
  174.5 166.1 %copy-start.36 = (f32[296]{0:T(512)}, f32[296]{0:T(512)S(1)}, u32[]{:S(2)}) copy-start(f32[296]{0:T(512)S(1)} %fusion.82) | copy-start | bytes 3556
  180.0 14.6 %collective-permute-start.7 = (bf16[64,4096]{1,0:T(8,128)(2,1)S(1)}, bf16[64,4096]{1,0:T(8,128)(2,1)S(1)}, u32[]{:S(2)}, u32[]{:S(2)}) collective-permute-start(bf16[64,4096]{1,0:T(8,128)(2,1)S(1)} %collective-permute-done.6), channel_id=1, source_target_pairs={{0,2},{2,4},{4,6},{6,8},{8,10},{10,12},{12,14},{14,16},{16,18},{18... | collective-permute-start | bytes 1572872 | tf_op jit(solution)/shard_map/ppermute | solution.py:26
  184.3 21.8 %copy-start.20 = (bf16[64,4096]{1,0:T(8,128)(2,1)S(1)}, bf16[64,4096]{1,0:T(8,128)(2,1)}, u32[]{:S(2)}) copy-start(bf16[64,4096]{1,0:T(8,128)(2,1)} %copy-done.19) | copy-start | bytes 1572868
  184.3 22.6 %copy-start.22 = (bf16[64,4096]{1,0:T(8,128)(2,1)S(1)}, bf16[64,4096]{1,0:T(8,128)(2,1)}, u32[]{:S(2)}) copy-start(bf16[64,4096]{1,0:T(8,128)(2,1)} %copy-done.21) | copy-start | bytes 1572868
  184.3 37.0 %copy-start.18 = (bf16[64,4096]{1,0:T(8,128)(2,1)S(1)}, bf16[64,4096]{1,0:T(8,128)(2,1)}, u32[]{:S(2)}) copy-start(bf16[64,4096]{1,0:T(8,128)(2,1)} %copy-done.17) | copy-start | bytes 1572868
  194.7 11.5 collective-permute-start.8
  206.1 15.2 %collective-permute-start.9 = (bf16[64,4096]{1,0:T(8,128)(2,1)S(1)}, bf16[64,4096]{1,0:T(8,128)(2,1)S(1)}, u32[]{:S(2)}, u32[]{:S(2)}) collective-permute-start(bf16[64,4096]{1,0:T(8,128)(2,1)S(1)} %collective-permute-done.8), channel_id=1, source_target_pairs={{0,2},{2,4},{4,6},{6,8},{8,10},{10,12},{12,14},{14,16},{16,18},{18... | collective-permute-start | bytes 1572872 | tf_op jit(solution)/shard_map/ppermute | solution.py:26
  221.3 11.3 collective-permute-start.10
  232.6 11.3 collective-permute-start.11
  243.9 11.3 collective-permute-start.12
  255.2 11.3 collective-permute-start.13
  266.5 11.8 collective-permute-start.14
  352.0 118.1 %copy-start.23 = (f32[256,512]{1,0:T(8,128)S(1)}, f32[256,512]{1,0:T(8,128)}, u32[]{:S(2)}) copy-start(f32[256,512]{1,0:T(8,128)} %param.25) | copy-start | bytes 1572868
  352.0 118.1 %copy-start.24 = (f32[256,512]{1,0:T(8,128)S(1)}, f32[256,512]{1,0:T(8,128)}, u32[]{:S(2)}) copy-start(f32[256,512]{1,0:T(8,128)} %param.31) | copy-start | bytes 1572868
  352.0 118.0 %reduce-scatter.41.cloned.1.call-start = ((), (), s32[]{:S(2)}) async-start(), calls=%async_computation.26 | async-start | bytes 786432 | tf_op jit(solution)/shard_map/reduce_scatter | solution.py:268
  453.6 102.1 %all-gather.18.cloned.1.call-start = ((), (), s32[]{:S(2)}) async-start(), calls=%async_computation.18 | async-start | bytes 8912896 | tf_op jit(solution)/shard_map/all_gather | solution.py:103
  481.3 301.8 %reduce-scatter.45.cloned.1.call-start = ((), (), s32[]{:S(2)}) async-start(), calls=%async_computation.28 | async-start | bytes 3637248
  608.2 179.6 %reduce-scatter.43.cloned.1.call-start = ((), (), s32[]{:S(2)}) async-start(), calls=%async_computation.27 | async-start | bytes 3637248
  703.9 115.0 %reduce-scatter.31.cloned.1.call-start = ((), (), s32[]{:S(2)}) async-start(), calls=%async_computation.21 | async-start | bytes 2228224 | tf_op jit(solution)/shard_map/reduce_scatter | solution.py:242
  708.8 154.6 %reduce-scatter.47.cloned.1.call-start = ((), (), s32[]{:S(2)}) async-start(), calls=%async_computation.29 | async-start | bytes 278528
  804.5 117.7 %reduce-scatter.51.cloned.1.call-start = ((), (), s32[]{:S(2)}) async-start(), calls=%async_computation.31 | async-start | bytes 278528
  806.7 222.1 %reduce-scatter.35.cloned.1.call-start = ((), (), s32[]{:S(2)}) async-start(), calls=%async_computation.23 | async-start | bytes 8912896 | tf_op jit(solution)/shard_map/reduce_scatter | solution.py:245
  818.8 44.7 %copy-start.10 = (bf16[2,296,1024]{2,1,0:T(8,128)(2,1)S(1)}, bf16[2,296,1024]{2,1,0:T(8,128)(2,1)}, u32[]{:S(2)}) copy-start(bf16[2,296,1024]{2,1,0:T(8,128)(2,1)} %copy.116) | copy-start | bytes 3637252
  818.8 44.7 %copy-start.42 = (f32[1,1024]{1,0:T(1,128)S(1)}, f32[1,1024]{1,0:T(1,128)}, u32[]{:S(2)}) copy-start(f32[1,1024]{1,0:T(1,128)} %copy-done.41) | copy-start | bytes 12292
  818.8 222.1 %reduce-scatter.33.cloned.1.call-start = ((), (), s32[]{:S(2)}) async-start(), calls=%async_computation.22 | async-start | bytes 196608 | tf_op jit(solution)/shard_map/reduce_scatter | solution.py:262
  819.4 233.6 %reduce-scatter.49.cloned.1.call-start = ((), (), s32[]{:S(2)}) async-start(), calls=%async_computation.30 | async-start | bytes 24576
  863.5 278.4 %reduce-scatter.27.cloned.1.call-start = ((), (), s32[]{:S(2)}) async-start(), calls=%async_computation.19 | async-start | bytes 6684672 | tf_op jit(solution)/shard_map/reduce_scatter | solution.py:239
  872.8 49.5 %copy-start.40 = (f32[1,1024]{1,0:T(1,128)S(1)}, f32[1,1024]{1,0:T(1,128)}, u32[]{:S(2)}) copy-start(f32[1,1024]{1,0:T(1,128)} %get-tuple-element.64) | copy-start | bytes 12292
  872.8 280.2 %reduce-scatter.53.cloned.1.call-start = ((), (), s32[]{:S(2)}) async-start(), calls=%async_computation.32 | async-start | bytes 24576
  922.2 247.5 %reduce-scatter.37.cloned.1.call-start = ((), (), s32[]{:S(2)}) async-start(), calls=%async_computation.24 | async-start | bytes 786432 | tf_op jit(solution)/shard_map/reduce_scatter | solution.py:265
  922.3 118.7 %copy-start.16 = (f32[64,512]{1,0:T(8,128)S(1)}, f32[64,512]{1,0:T(8,128)}, u32[]{:S(2)}) copy-start(f32[64,512]{1,0:T(8,128)} %param.23) | copy-start | bytes 393220
  922.3 118.7 %copy-start.27 = (f32[64,512]{1,0:T(8,128)S(1)}, f32[64,512]{1,0:T(8,128)}, u32[]{:S(2)}) copy-start(f32[64,512]{1,0:T(8,128)} %param.29) | copy-start | bytes 393220
  922.3 118.6 %copy-start.28 = (f32[64,512]{1,0:T(8,128)S(1)}, f32[64,512]{1,0:T(8,128)}, u32[]{:S(2)}) copy-start(f32[64,512]{1,0:T(8,128)} %param.35) | copy-start | bytes 393220
  1028.9 156.3 %reduce-scatter.29.cloned.1.call-start = ((), (), s32[]{:S(2)}) async-start(), calls=%async_computation.20 | async-start | bytes 589824 | tf_op jit(solution)/shard_map/reduce_scatter | solution.py:259
  1042.6 99.3 %copy-start.45 = (f32[2,32]{1,0:T(2,128)S(1)}, f32[2,32]{1,0:T(2,128)}, u32[]{:S(2)}) copy-start(f32[2,32]{1,0:T(2,128)} %param.26) | copy-start | bytes 772
  1042.6 99.3 %copy-start.46 = (f32[2,32]{1,0:T(2,128)S(1)}, f32[2,32]{1,0:T(2,128)}, u32[]{:S(2)}) copy-start(f32[2,32]{1,0:T(2,128)} %param.32) | copy-start | bytes 772
  1042.6 99.3 %copy-start.47 = (f32[2,32]{1,0:T(2,128)S(1)}, f32[2,32]{1,0:T(2,128)}, u32[]{:S(2)}) copy-start(f32[2,32]{1,0:T(2,128)} %param.38) | copy-start | bytes 772
  1042.6 111.1 %copy-start.29 = (f32[10,32]{1,0:T(8,128)S(1)}, f32[10,32]{1,0:T(8,128)}, u32[]{:S(2)}) copy-start(f32[10,32]{1,0:T(8,128)} %param.27) | copy-start | bytes 3844
  1042.6 111.1 %copy-start.38 = (f32[10,32]{1,0:T(8,128)S(1)}, f32[10,32]{1,0:T(8,128)}, u32[]{:S(2)}) copy-start(f32[10,32]{1,0:T(8,128)} %param.33) | copy-start | bytes 3844
  1042.7 111.1 %copy-start.39 = (f32[10,32]{1,0:T(8,128)S(1)}, f32[10,32]{1,0:T(8,128)}, u32[]{:S(2)}) copy-start(f32[10,32]{1,0:T(8,128)} %param.39) | copy-start | bytes 3844
  1042.7 127.0 %copy-start.8 = (f32[64,2048]{1,0:T(8,128)S(1)}, f32[64,2048]{1,0:T(8,128)}, u32[]{:S(2)}) copy-start(f32[64,2048]{1,0:T(8,128)} %param.24) | copy-start | bytes 1572868
  1042.7 127.0 %copy-start.13 = (f32[64,2048]{1,0:T(8,128)S(1)}, f32[64,2048]{1,0:T(8,128)}, u32[]{:S(2)}) copy-start(f32[64,2048]{1,0:T(8,128)} %param.30) | copy-start | bytes 1572868
  1042.7 127.0 %copy-start.14 = (f32[64,2048]{1,0:T(8,128)S(1)}, f32[64,2048]{1,0:T(8,128)}, u32[]{:S(2)}) copy-start(f32[64,2048]{1,0:T(8,128)} %param.36) | copy-start | bytes 1572868
  1047.1 138.1 %copy-start.9 = (f32[64,1536]{1,0:T(8,128)S(1)}, f32[64,1536]{1,0:T(8,128)}, u32[]{:S(2)}) copy-start(f32[64,1536]{1,0:T(8,128)} %param.22) | copy-start | bytes 1179652
  1047.1 138.1 %copy-start.25 = (f32[64,1536]{1,0:T(8,128)S(1)}, f32[64,1536]{1,0:T(8,128)}, u32[]{:S(2)}) copy-start(f32[64,1536]{1,0:T(8,128)} %param.28) | copy-start | bytes 1179652
  1047.1 138.1 %copy-start.26 = (f32[64,1536]{1,0:T(8,128)S(1)}, f32[64,1536]{1,0:T(8,128)}, u32[]{:S(2)}) copy-start(f32[64,1536]{1,0:T(8,128)} %param.34) | copy-start | bytes 1179652
  (23 other events, 166.7 us)
Sparse Core Ops, SparseCore 0:
  17.2 63.0 all-gather.9
  90.8 35.4 all-gather.11
  127.9 37.4 all-gather.13
  174.2 46.5 all-gather.15
  352.1 101.4 reduce-scatter.38
  455.7 14.2 reduce-scatter.40
  481.4 74.2 all-gather.17
  608.4 34.0 reduce-scatter.44
  704.0 34.8 reduce-scatter.42
  742.4 62.1 reduce-scatter.30
  808.7 54.6 reduce-scatter.46
  867.4 54.7 reduce-scatter.50
  926.2 102.5 reduce-scatter.34
  1030.9 9.9 reduce-scatter.32
  1043.0 9.9 reduce-scatter.48
  1056.7 85.0 reduce-scatter.26
  1143.9 9.0 reduce-scatter.52
  1155.1 14.6 reduce-scatter.36
  1172.0 13.1 reduce-scatter.28
